TPU v7x, 32 devices: a whole 2x2x4 slice. The times are simulated.
32 devices in a mesh: dp: 16 (over z, y, x), tensor: 2 (over core).
Axes of the slice: x: 2, y: 2, z: 4, core: 2. Of those that a mesh axis runs over, the one named last changes fastest.
Arguments:
- tokens: bfloat16 [8192, 1024], P(('dp', 'tensor')), may hold values from -6 to 6
- segment_ids: int32 [8192], P('dp'), may hold values from 0 to 2, as said below
- positions: int32 [8192], P('dp'), may hold values from 0 to 2047, as said below
- norm1_gain: float32 [1024], replicated, may hold values from 0.25 to 1.75
- qkv_weight: bfloat16 [1024, 3, 1024], P(None, None, 'tensor'), may hold values from -0.1875 to 0.1875
- out_weight: bfloat16 [1024, 1024], P('tensor'), may hold values from -1.5 to 1.5
- norm2_gain: float32 [1024], replicated, may hold values from 0.25 to 1.75
- mlp_in_weight: bfloat16 [1024, 2, 2624], P(None, None, 'tensor'), may hold values from -0.1875 to 0.1875
- mlp_out_weight: bfloat16 [2624, 1024], P('tensor'), may hold values from -0.125 to 0.125
- cotangent: bfloat16 [8192, 1024], P(('dp', 'tensor')), may hold values from -6 to 6
Outputs:
- output: bfloat16 [8192, 1024], P(('dp', 'tensor'))
- input_grad: bfloat16 [8192, 1024], P(('dp', 'tensor'))
- norm1_gain_grad: float32 [1024], replicated
- qkv_weight_grad: float32 [1024, 3, 1024], P(None, None, 'tensor')
- out_weight_grad: float32 [1024, 1024], P('tensor')
- norm2_gain_grad: float32 [1024], replicated
- mlp_in_weight_grad: float32 [1024, 2, 2624], P(None, None, 'tensor')
- mlp_out_weight_grad: float32 [2624, 1024], P('tensor')
Inputs may be any that keep to these rules, and one draw needn't show every extreme that they name: Within each sequence of 512 tokens segment_ids never falls and rises by at most one per step; tokens attend only to tokens of the same sequence and segment. Inside a segment positions rise by one per token; a segment that begins a sequence starts at a position of at most 1536, every later one starts at 0.
All inputs are finite; a program needn't handle non-finite values.
Results may differ from a plain program's by a relative error of at most 0.02.
Values may be sent and summed in bfloat16 or wider, within the bound.
A program may use at most 128 MiB of HBM per device.

v0:
```python
import math
import jax
import jax.numpy as jnp
from jax import lax
from jax.sharding import PartitionSpec as P

HEAD_DIM = 64
SEQ_LEN = 512
EPS = 1e-05
THETA = 160000.0
NEG_FILL = -1e30
INV_ROOT_TWO_PI = 0.3989422804014327


def norm_rows(rows):
    centered = rows - jnp.mean(rows, axis=-1, keepdims=True)
    inv_spread = lax.rsqrt(jnp.mean(centered * centered, axis=-1, keepdims=True) + EPS)
    return (centered * inv_spread, inv_spread)


def norm_back(grad_rows, normed, inv_spread):
    return inv_spread * (
        grad_rows
        - jnp.mean(grad_rows, axis=-1, keepdims=True)
        - normed * jnp.mean(grad_rows * normed, axis=-1, keepdims=True)
    )


def rope_tables(position_ids):
    half_dim = HEAD_DIM // 2
    freqs = jnp.exp(-math.log(THETA) * (jnp.arange(half_dim, dtype=jnp.float32) * 2.0 / HEAD_DIM))
    angles = position_ids.astype(jnp.float32)[:, None] * freqs[None, :]
    cos_table = jnp.concatenate([jnp.cos(angles), jnp.cos(angles)], axis=-1)[:, None, :]
    sin_table = jnp.concatenate([jnp.sin(angles), jnp.sin(angles)], axis=-1)[:, None, :]
    return (cos_table, sin_table)


def rotate(values, cos_table, sin_table):
    half_dim = HEAD_DIM // 2
    turned = jnp.concatenate([-values[..., half_dim:], values[..., :half_dim]], axis=-1)
    return values * cos_table + turned * sin_table


def unrotate(grads, cos_table, sin_table):
    half_dim = HEAD_DIM // 2
    weighted = grads * sin_table
    turned = jnp.concatenate([weighted[..., half_dim:], -weighted[..., :half_dim]], axis=-1)
    return grads * cos_table + turned


def attend(query, key_rot, value, seg_row):
    scale = HEAD_DIM ** (-0.5)
    scores = jnp.einsum("qhd,khd->hqk", query, key_rot, preferred_element_type=jnp.float32) * scale
    allowed = (seg_row[:, None] == seg_row[None, :])[None]
    scores = jnp.where(allowed, scores, NEG_FILL)
    row_max = jnp.max(scores, axis=-1)
    expd = jnp.exp(scores - row_max[..., None])
    total = jnp.sum(expd, axis=-1)
    log_total = row_max + jnp.log(total)
    probs = (expd / total[..., None]).astype(jnp.bfloat16)
    attended = jnp.einsum("hqk,khd->qhd", probs, value, preferred_element_type=jnp.float32)
    return (attended.astype(jnp.bfloat16), log_total)


def attend_back(query, key_rot, value, attended, grad_out, log_total, seg_row):
    scale = HEAD_DIM ** (-0.5)
    scores = jnp.einsum("qhd,khd->hqk", query, key_rot, preferred_element_type=jnp.float32) * scale
    allowed = (seg_row[:, None] == seg_row[None, :])[None]
    probs = jnp.where(allowed, jnp.exp(scores - log_total[..., None]), 0.0)
    probs_low = probs.astype(jnp.bfloat16)
    grad_value = jnp.einsum("hqk,qhd->khd", probs_low, grad_out, preferred_element_type=jnp.float32)
    grad_probs = jnp.einsum("qhd,khd->hqk", grad_out, value, preferred_element_type=jnp.float32)
    delta = jnp.sum(grad_out.astype(jnp.float32) * attended.astype(jnp.float32), axis=-1).T
    grad_scores = (probs * (grad_probs - delta[..., None]) * scale).astype(jnp.bfloat16)
    grad_query = jnp.einsum(
        "hqk,khd->qhd", grad_scores, key_rot, preferred_element_type=jnp.float32
    )
    grad_key = jnp.einsum("hqk,qhd->khd", grad_scores, query, preferred_element_type=jnp.float32)
    return (grad_query, grad_key, grad_value)


def contract_rows(left, right):
    return lax.dot_general(
        left, right, (((0,), (0,)), ((), ())), preferred_element_type=jnp.float32
    )


def contract_cols(left, right):
    return lax.dot_general(
        left, right, (((1,), (1,)), ((), ())), preferred_element_type=jnp.float32
    )


def per_device(
    tokens,
    segment_ids,
    positions,
    norm1_gain,
    qkv_weight,
    out_weight,
    norm2_gain,
    mlp_in_weight,
    mlp_out_weight,
    cotangent,
):
    local_len = segment_ids.shape[0]
    seq_count = local_len // SEQ_LEN
    head_width = out_weight.shape[0]
    head_count = head_width // HEAD_DIM

    def split_seq(array):
        return array.reshape((seq_count, SEQ_LEN) + array.shape[1:])

    token_f32 = tokens.astype(jnp.float32)
    normed_one, spread_one = norm_rows(token_f32)
    attn_in = (normed_one * norm1_gain).astype(jnp.bfloat16)
    full_one = lax.all_gather(attn_in, "tensor", axis=0, tiled=True)
    projected = jnp.einsum("td,dch->tch", full_one, qkv_weight, preferred_element_type=jnp.float32)
    cos_table, sin_table = rope_tables(positions)
    query = rotate(
        projected[:, 0].reshape(local_len, head_count, HEAD_DIM), cos_table, sin_table
    ).astype(jnp.bfloat16)
    key_rot = rotate(
        projected[:, 1].reshape(local_len, head_count, HEAD_DIM), cos_table, sin_table
    ).astype(jnp.bfloat16)
    value = projected[:, 2].reshape(local_len, head_count, HEAD_DIM).astype(jnp.bfloat16)

    def attend_item(item):
        return attend(item[0], item[1], item[2], item[3])

    attended, log_total = lax.map(
        attend_item,
        (split_seq(query), split_seq(key_rot), split_seq(value), split_seq(segment_ids)),
    )
    attended = attended.reshape(local_len, head_count, HEAD_DIM)
    attn_flat = attended.reshape(local_len, head_width)
    resid_mid = token_f32 + lax.psum_scatter(
        jnp.dot(attn_flat, out_weight, preferred_element_type=jnp.float32),
        "tensor",
        scatter_dimension=0,
        tiled=True,
    )
    normed_two, spread_two = norm_rows(resid_mid)
    mlp_in = (normed_two * norm2_gain).astype(jnp.bfloat16)
    full_two = lax.all_gather(mlp_in, "tensor", axis=0, tiled=True)
    gate_up = jnp.einsum("td,dch->tch", full_two, mlp_in_weight, preferred_element_type=jnp.float32)
    gate_pre = gate_up[:, 0]
    up_part = gate_up[:, 1]
    activated = jax.nn.gelu(gate_pre, approximate=False)
    hidden = (activated * up_part).astype(jnp.bfloat16)
    output = (
        resid_mid
        + lax.psum_scatter(
            jnp.dot(hidden, mlp_out_weight, preferred_element_type=jnp.float32).astype(
                jnp.bfloat16
            ),
            "tensor",
            scatter_dimension=0,
            tiled=True,
        ).astype(jnp.float32)
    ).astype(jnp.bfloat16)
    full_cot = lax.all_gather(cotangent, "tensor", axis=0, tiled=True)
    grad_w2 = contract_rows(hidden, full_cot)
    grad_hidden = contract_cols(full_cot, mlp_out_weight)
    slope = (
        0.5 * (1.0 + jax.scipy.special.erf(gate_pre / math.sqrt(2.0)))
        + gate_pre * jnp.exp(-0.5 * gate_pre * gate_pre) * INV_ROOT_TWO_PI
    )
    grad_gu = jnp.stack([grad_hidden * up_part * slope, grad_hidden * activated], axis=1).astype(
        jnp.bfloat16
    )
    grad_w1 = contract_rows(full_two, grad_gu)
    grad_mlp_in = lax.psum_scatter(
        jnp.einsum("tch,dch->td", grad_gu, mlp_in_weight, preferred_element_type=jnp.float32),
        "tensor",
        scatter_dimension=0,
        tiled=True,
    )
    grad_gain_two = jnp.sum(grad_mlp_in * normed_two, axis=0)
    grad_mid = cotangent.astype(jnp.float32) + norm_back(
        grad_mlp_in * norm2_gain, normed_two, spread_two
    )
    full_mid = lax.all_gather(grad_mid.astype(jnp.bfloat16), "tensor", axis=0, tiled=True)
    grad_wo = contract_rows(attn_flat, full_mid)
    grad_att = (
        contract_cols(full_mid, out_weight)
        .astype(jnp.bfloat16)
        .reshape(local_len, head_count, HEAD_DIM)
    )

    def back_item(item):
        return attend_back(item[0], item[1], item[2], item[3], item[4], item[5], item[6])

    grad_query, grad_key, grad_value = lax.map(
        back_item,
        (
            split_seq(query),
            split_seq(key_rot),
            split_seq(value),
            split_seq(attended),
            split_seq(grad_att),
            log_total,
            split_seq(segment_ids),
        ),
    )
    grad_query = grad_query.reshape(local_len, head_count, HEAD_DIM)
    grad_key = grad_key.reshape(local_len, head_count, HEAD_DIM)
    grad_value = grad_value.reshape(local_len, head_count, HEAD_DIM)
    grad_proj = jnp.stack(
        [
            unrotate(grad_query, cos_table, sin_table).reshape(local_len, head_width),
            unrotate(grad_key, cos_table, sin_table).reshape(local_len, head_width),
            grad_value.reshape(local_len, head_width),
        ],
        axis=1,
    ).astype(jnp.bfloat16)
    grad_wqkv = contract_rows(full_one, grad_proj)
    grad_attn_in = lax.psum_scatter(
        jnp.einsum("tch,dch->td", grad_proj, qkv_weight, preferred_element_type=jnp.float32).astype(
            jnp.bfloat16
        ),
        "tensor",
        scatter_dimension=0,
        tiled=True,
    ).astype(jnp.float32)
    grad_gain_one = jnp.sum(grad_attn_in * normed_one, axis=0)
    input_grad = (grad_mid + norm_back(grad_attn_in * norm1_gain, normed_one, spread_one)).astype(
        jnp.bfloat16
    )
    grad_gain_one, grad_gain_two = lax.psum((grad_gain_one, grad_gain_two), ("dp", "tensor"))
    grad_wqkv, grad_wo, grad_w1, grad_w2 = (
        lax.psum(grad_wqkv.astype(jnp.bfloat16), "dp").astype(jnp.float32),
        lax.psum(grad_wo.astype(jnp.bfloat16), "dp").astype(jnp.float32),
        lax.psum(grad_w1.astype(jnp.bfloat16), "dp").astype(jnp.float32),
        lax.psum(grad_w2.astype(jnp.bfloat16), "dp").astype(jnp.float32),
    )
    return (output, input_grad, grad_gain_one, grad_wqkv, grad_wo, grad_gain_two, grad_w1, grad_w2)


def solution(mesh):
    return jax.shard_map(
        per_device,
        mesh=mesh,
        in_specs=(
            P(("dp", "tensor"), None),
            P("dp"),
            P("dp"),
            P(),
            P(None, None, "tensor"),
            P("tensor", None),
            P(),
            P(None, None, "tensor"),
            P("tensor", None),
            P(("dp", "tensor"), None),
        ),
        out_specs=(
            P(("dp", "tensor"), None),
            P(("dp", "tensor"), None),
            P(),
            P(None, None, "tensor"),
            P("tensor", None),
            P(),
            P(None, None, "tensor"),
            P("tensor", None),
        ),
        check_vma=False,
    )
```

profile of v0, /device:TPU:0, one launch (start us, length us, event | category | flops | bytes accessed | tf_op | source)
XLA Modules:
  0.0 558.1 jit_solution(8671256231642317584)
XLA Ops:
  14.6 9.9 %all-gather.5.cloned.1.call-done = bf16[512,1024]{1,0:T(8,128)(2,1)} async-done(((bf16[256,1024]{1,0:T(8,128)(2,1)}), bf16[512,1024]{1,0:T(8,128)(2,1)}) %all-gather.5.cloned.1.call-update) | async-done | bytes 1048592 | tf_op jit(solution)/shard_map/all_gather | solution.py:117
  24.5 3.1 fusion.54
  39.8 11.0 %reduce-scatter.5.cloned.1.call-done = f32[256,1024]{1,0:T(8,128)} async-done(((f32[512,1024]{1,0:T(8,128)}), f32[256,1024]{1,0:T(8,128)}) %reduce-scatter.5.cloned.1.call-update) | async-done | bytes 1048592 | tf_op jit(solution)/shard_map/reduce_scatter | solution.py:137
  56.1 9.4 %all-gather.7.cloned.1.call-done = bf16[512,1024]{1,0:T(8,128)(2,1)} async-done(((bf16[256,1024]{1,0:T(8,128)(2,1)}), bf16[512,1024]{1,0:T(8,128)(2,1)}) %all-gather.7.cloned.1.call-update) | async-done | bytes 1048592 | tf_op jit(solution)/shard_map/all_gather | solution.py:145
  65.5 8.3 %fusion.51 = f32[512,2,1312]{0,2,1:T(8,128)} fusion(bf16[1024,2,1312]{0,2,1:T(8,128)(2,1)} %param.17, bf16[512,1024]{1,0:T(8,128)(2,1)} %all-gather.7.cloned.1.call-done), kind=kOutput, calls=%fused_computation.88 | convolution fusion | flops 2751463424 | bytes 11796480 | tf_op jit(solution)/shard_map/td,dch->tch/dot_general | solution.py:146
  73.7 3.4 all-gather.9.cloned.1.call-done
  77.1 11.4 %fusion.23 = (bf16[512,1,1312]{0,2,1:T(8,128)(2,1)S(1)}, f32[512,1312]{0,1:T(8,128)}, bf16[512,1,1312]{0,2,1:T(8,128)(2,1)S(1)}) fusion(f32[512,2,1312]{0,2,1:T(8,128)} %fusion.51, bf16[512,1024]{1,0:T(8,128)(2,1)} %all-gather.9.cloned.1.call-done, bf16[1312,1024]{1,0:T(8,128)(2,1)} %param.18), kind=kOutput, calls=%fused_computation.54 | convolution fusion | flops 1427456000 | bytes 14483456 | tf_op jit(solution)/shard_map/dot_general | solution.py:89
  90.0 7.0 %fusion.22 = f32[512,1024]{1,0:T(8,128)} fusion(bf16[1024,2,1312]{0,2,1:T(8,128)(2,1)} %param.17, bf16[512,1,1312]{0,2,1:T(8,128)(2,1)S(1)} %get-tuple-element.76, bf16[512,1,1312]{0,2,1:T(8,128)(2,1)S(1)} %get-tuple-element.80), kind=kOutput, calls=%fused_computation.45 | convolution fusion | flops 2752806912 | bytes 10158080 | tf_op jit(solution)/shard_map/tch,dch->td/dot_general | solution.py:174
  97.1 3.2 multiply_convert_fusion.2
  104.2 3.9 reduce-scatter.9.cloned.1.call-done
  112.0 8.6 %reduce-scatter.7.cloned.1.call-done = bf16[256,1024]{1,0:T(8,128)(2,1)} async-done(((bf16[512,1024]{1,0:T(8,128)(2,1)}), bf16[256,1024]{1,0:T(8,128)(2,1)}) %reduce-scatter.7.cloned.1.call-update) | async-done | bytes 524304 | tf_op jit(solution)/shard_map/reduce_scatter | solution.py:153
  120.5 3.7 fusion.64
  125.8 8.9 %all-gather.11.cloned.1.call-done = bf16[512,1024]{1,0:T(8,128)(2,1)} async-done(((bf16[256,1024]{1,0:T(8,128)(2,1)}), bf16[512,1024]{1,0:T(8,128)(2,1)}) %all-gather.11.cloned.1.call-update) | async-done | bytes 1048592 | tf_op jit(solution)/shard_map/all_gather | solution.py:183
  137.7 6.1 %fusion.29 = bf16[8,64,512]{2,1,0:T(8,128)(2,1)} fusion(bf16[512,8,64]{0,2,1:T(8,128)(2,1)S(1)} %bitcast.94, f32[8,512,512]{1,2,0:T(8,128)} %copy-done.1, f32[8,512]{1,0:T(8,128)S(1)} %copy-done.29, pred[512,512]{0,1:T(8,128)(4,1)S(1)} %broadcast_compare_fusion), kind=kOutput, calls=%fused_computation.62 | convolution fusion | flops 277086208 | bytes 9715712 | tf_op jit(solution)/shard_map/while/body/eval_jaxpr/hqk,qhd->khd/dot_general | solution.py:71
  145.9 6.6 %multiply_convert_fusion = bf16[8,512,512]{1,2,0:T(8,128)(2,1)S(1)} fusion(f32[8,512,512]{1,2,0:T(8,128)} %copy-done.1, f32[8,512]{1,0:T(8,128)} %bitcast.96, f32[8,512]{1,0:T(8,128)S(1)} %copy-done.29, pred[512,512]{0,1:T(8,128)(4,1)S(1)} %broadcast_compare_fusion, bf16[512,8,64]{0,2,1:T(8,128)(2,1)} %bitcast.95, bf16[512,8,64]{0,2,1:T(8,128)(2,1)} %bitcast.92), kind=kOutput, calls=%fused_computation | convolution fusion | flops 283115520 | bytes 13926400 | tf_op jit(solution)/shard_map/while/body/eval_jaxpr/qhd,khd->hqk/dot_general | solution.py:72
  161.3 4.2 bitcast_convert_fusion
  165.8 4.9 convolution_convert_fusion.1
  170.7 4.7 convolution_convert_fusion
  177.2 3.5 convolution_convert_fusion.2
  183.1 43.8 %all-reduce = (f32[1024]{0:T(1024)}, f32[1024]{0:T(1024)}) all-reduce(f32[1024]{0:T(1024)S(1)} %get-tuple-element.54, f32[1024]{0:T(1024)S(1)} %copy-done.28), channel_id=1, replica_groups=mesh['dp'=16,'tensor'=2] {'dp','tensor'}, use_global_device_ids=true, to_apply=%region_16.17 | all-reduce | flops 2048 | bytes 16384 | tf_op jit(solution)/shard_map/psum | solution.py:230
  229.7 305.8 %all-reduce.4.cloned.1.call-done = (bf16[1024,3,512]{2,0,1:T(8,128)(2,1)}, bf16[512,1024]{1,0:T(8,128)(2,1)}, bf16[1024,2,1312]{0,2,1:T(8,128)(2,1)}, bf16[1312,1024]{1,0:T(8,128)(2,1)}) async-done(((bf16[1024,3,512]{2,0,1:T(8,128)(2,1)}, bf16[512,1024]{1,0:T(8,128)(2,1)}, bf16[1024,2,1312]{0,2,1:T(8,128)(2,1)}, bf16[1312,1024]{1,0:T(8,128)(2,1)}), (bf16[1024,3,512]{2,0,1:T(8,128)(2,1)}, ...) | async-done | bytes 12255248 | tf_op jit(solution)/shard_map/psum | solution.py:232
  535.6 5.6 %convert_element_type.130 = f32[1024,3,512]{2,0,1:T(8,128)} convert(bf16[1024,3,512]{2,0,1:T(8,128)(2,1)} %get-tuple-element.59) | non-fusion elementwise | flops 1572864 | bytes 9437184 | tf_op jit(solution)/shard_map/convert_element_type | solution.py:232
  542.8 5.5 convert_element_type.134
  548.3 3.1 convert_element_type.136
  (147 shorter events, 58.1 us)
Async XLA Ops:
  7.2 17.4 %copy-start = (bf16[1024,3,512]{2,0,1:T(8,128)(2,1)S(1)}, bf16[1024,3,512]{2,0,1:T(8,128)(2,1)}, u32[]{:S(2)}) copy-start(bf16[1024,3,512]{2,0,1:T(8,128)(2,1)} %param.14) | copy-start | bytes 9437188
  7.2 7.2 %copy-start.30 = (s32[512]{0:T(512)S(1)}, s32[512]{0:T(512)}, u32[]{:S(2)}) copy-start(s32[512]{0:T(512)} %param.11) | copy-start | bytes 6148
  7.2 17.3 %all-gather.5.cloned.1.call-start = ((), (), s32[]{:S(2)}) async-start(), calls=%async_computation.4 | async-start | bytes 1572864 | tf_op jit(solution)/shard_map/all_gather | solution.py:117
  12.6 38.2 %reduce-scatter.5.cloned.1.call-start = ((), (), s32[]{:S(2)}) async-start(), calls=%async_computation.5 | async-start | bytes 3145728 | tf_op jit(solution)/shard_map/reduce_scatter | solution.py:137
  27.7 5.0 copy-start.15
  39.8 25.7 %all-gather.7.cloned.1.call-start = ((), (), s32[]{:S(2)}) async-start(), calls=%async_computation.6 | async-start | bytes 1572864 | tf_op jit(solution)/shard_map/all_gather | solution.py:145
  55.0 22.1 %all-gather.9.cloned.1.call-start = ((), (), s32[]{:S(2)}) async-start(), calls=%async_computation.8 | async-start | bytes 1572864 | tf_op jit(solution)/shard_map/all_gather | solution.py:162
  55.6 52.6 %reduce-scatter.9.cloned.1.call-start = ((), (), s32[]{:S(2)}) async-start(), calls=%async_computation.9 | async-start | bytes 3145728 | tf_op jit(solution)/shard_map/reduce_scatter | solution.py:173
  97.1 23.4 %reduce-scatter.7.cloned.1.call-start = ((), (), s32[]{:S(2)}) async-start(), calls=%async_computation.7 | async-start | bytes 1572864 | tf_op jit(solution)/shard_map/reduce_scatter | solution.py:153
  104.2 30.4 %all-gather.11.cloned.1.call-start = ((), (), s32[]{:S(2)}) async-start(), calls=%async_computation.10 | async-start | bytes 1572864 | tf_op jit(solution)/shard_map/all_gather | solution.py:183
  124.2 56.5 %reduce-scatter.11.cloned.1.call-start = ((), (), s32[]{:S(2)}) async-start(), calls=%async_computation.11 | async-start | bytes 1572864 | tf_op jit(solution)/shard_map/reduce_scatter | solution.py:218
  125.8 11.9 %copy-start.29 = (f32[8,512]{1,0:T(8,128)S(1)}, f32[8,512]{1,0:T(8,128)}, u32[]{:S(2)}) copy-start(f32[8,512]{1,0:T(8,128)} %log_add_fusion) | copy-start | bytes 49156
  137.7 6.1 %copy-start.35 = (bf16[512,512]{0,1:T(8,128)(2,1)}, bf16[512,512]{0,1:T(8,128)(2,1)S(1)}, u32[]{:S(2)}) copy-start(bf16[512,512]{0,1:T(8,128)(2,1)S(1)} %get-tuple-element.103) | copy-start | bytes 1572868
  145.9 6.6 %copy-start.6 = (bf16[512,8,64]{0,2,1:T(8,128)(2,1)S(1)}, bf16[512,8,64]{0,2,1:T(8,128)(2,1)}, u32[]{:S(2)}) copy-start(bf16[512,8,64]{0,2,1:T(8,128)(2,1)} %copy-done.5) | copy-start | bytes 1572868
  165.5 370.0 %all-reduce.4.cloned.1.call-start = ((), (), s32[]{:S(2)}) async-start(), calls=%async_computation.12 | async-start | bytes 24510464 | tf_op jit(solution)/shard_map/psum | solution.py:232
  165.8 4.9 copy-start.33
  165.8 4.9 copy-start.37
  165.8 4.9 copy-start.39
  170.7 4.7 copy-start.14
  170.7 4.7 copy-start.34
  535.6 7.2 %slice-start = ((s8[5373952]{0:T(1024)(128)(4,1)}), s8[4194304]{0:T(1024)(128)(4,1)S(1)}, s32[]{:S(2)}) async-start(s8[5373952]{0:T(1024)(128)(4,1)} %bitcast.85), calls=%async_computation.13 | async-start | bytes 8388608
  535.6 5.7 %copy-start.12 = (bf16[512,1024]{1,0:T(8,128)(2,1)S(1)}, bf16[512,1024]{1,0:T(8,128)(2,1)}, u32[]{:S(2)}) copy-start(bf16[512,1024]{1,0:T(8,128)(2,1)} %get-tuple-element.60) | copy-start | bytes 3145732
  535.6 7.2 %slice-start.1 = ((s8[5373952]{0:T(1024)(128)(4,1)}), s8[1179648]{0:T(1024)(128)(4,1)S(1)}, s32[]{:S(2)}) async-start(s8[5373952]{0:T(1024)(128)(4,1)} %bitcast.85), calls=%async_computation.14 | async-start | bytes 2359296
  542.8 5.5 copy-start.7
  (27 other events, 45.2 us)
Sparse Core Ops, SparseCore 0:
  12.7 11.7 all-gather.4
  39.9 10.9 reduce-scatter.4
  55.1 10.2 all-gather.6
  66.9 10.1 all-gather.8
  97.2 10.9 reduce-scatter.8
  110.8 9.6 reduce-scatter.6
  124.3 10.2 all-gather.10
  165.6 9.5 reduce-scatter.10
  182.2 353.2 all-reduce.3
where the time goes:
time: 566 us; the launch traced here: 558 us
  waiting for transfers between devices  362 us (64%)
  matrix products  75.6 us (13%)
  other arithmetic  46.2 us (8%)
  blocking collectives  43.8 us (8%)
  local copies, waits for them, and re-layouts  15.2 us (3%)
  between operations  14.5 us (3%)
    psum x1, waiting for transfers between devices, per_device(): lax.psum(grad_wqkv.astype(jnp.bfloat16), 'dp').astype(jnp.float32)  306 us
    psum x1, blocking collectives, per_device(): lax.psum((grad_gain_one, grad_gain_two), ('dp', 'tensor'))  43.8 us
    dot_general x4, matrix products, contract_rows(): lax.dot_general(left, right, (((0,), (0,)), ((), ())), preferred_element_...  14.8 us
    dot_general x2, matrix products, contract_cols(): lax.dot_general(left, right, (((1,), (1,)), ((), ())), preferred_element_...  14.4 us
  transfers between devices with their start and end apart: 9, of which 8 were waited for; matrix products, arithmetic and copies ran while one was open for 7% of the time, Pallas kernels for 0%

commit v1 on v0

--- a/solution.py
+++ b/solution.py
@@ -229,7 +229,7 @@
     )
     grad_gain_one, grad_gain_two = lax.psum((grad_gain_one, grad_gain_two), ("dp", "tensor"))
     grad_wqkv, grad_wo, grad_w1, grad_w2 = (
-        lax.psum(grad_wqkv.astype(jnp.bfloat16), "dp").astype(jnp.float32),
+        jnp.sum(lax.all_gather(grad_wqkv.astype(jnp.bfloat16), "dp"), axis=0).astype(jnp.float32),
         lax.psum(grad_wo.astype(jnp.bfloat16), "dp").astype(jnp.float32),
         lax.psum(grad_w1.astype(jnp.bfloat16), "dp").astype(jnp.float32),
         lax.psum(grad_w2.astype(jnp.bfloat16), "dp").astype(jnp.float32),

time: 566 us -> 1010 us (1.78)
  waiting for transfers between devices: 362 us -> 779 us
  other arithmetic: 46.2 us -> 66.8 us
    all_gather x0 -> x1, waiting for transfers between devices: none -> 498 us  [per_device(): lax.all_gather(grad_wqkv.astype(jnp.bfloat16), 'dp')]
    psum x1, waiting for transfers between devices: 306 us -> 225 us  [per_device(): lax.psum(grad_wo.astype(jnp.bfloat16), 'dp').astype(jnp.float32)]
    reduce_sum x0 -> x1, other arithmetic: none -> 18.3 us  [per_device(): jnp.sum(lax.all_gather(grad_wqkv.astype(jnp.bfloat16), 'dp'), axis=0)]
  transfers between devices with their start and end apart: 9 -> 10, of which waited for: 8 -> 9; matrix products, arithmetic and copies ran while one was open for 7% -> 5% of each run, Pallas kernels for 0% -> 0%
where the time goes in v1:
time: 1010 us; the launch traced here: 999 us
  waiting for transfers between devices  779 us (77%)
  matrix products  77 us (8%)
  other arithmetic  66.8 us (7%)
  blocking collectives  44.2 us (4%)
  local copies, waits for them, and re-layouts  15.2 us (2%)
  between operations  14.8 us (1%)
    all_gather x1, waiting for transfers between devices, per_device(): lax.all_gather(grad_wqkv.astype(jnp.bfloat16), 'dp')  498 us
    psum x1, waiting for transfers between devices, per_device(): lax.psum(grad_wo.astype(jnp.bfloat16), 'dp').astype(jnp.float32)  225 us
    psum x1, blocking collectives, per_device(): lax.psum((grad_gain_one, grad_gain_two), ('dp', 'tensor'))  44.2 us
  transfers between devices with their start and end apart: 10, of which 9 were waited for; matrix products, arithmetic and copies ran while one was open for 5% of the time, Pallas kernels for 0%

profile of v1, /device:TPU:0, one launch (start us, length us, event | category | flops | bytes accessed | tf_op | source)
XLA Modules:
  0.0 998.8 jit_solution(17525784125295788161)
XLA Ops:
  14.7 9.9 all-gather.7.cloned.1.call-done
  39.9 11.0 %reduce-scatter.5.cloned.1.call-done = f32[256,1024]{1,0:T(8,128)} async-done(((f32[512,1024]{1,0:T(8,128)}), f32[256,1024]{1,0:T(8,128)}) %reduce-scatter.5.cloned.1.call-update) | async-done | bytes 1048592 | tf_op jit(solution)/shard_map/reduce_scatter | solution.py:137
  56.2 9.3 all-gather.9.cloned.1.call-done
  65.5 8.2 fusion.51
  73.8 3.4 all-gather.11.cloned.1.call-done
  77.2 11.4 %fusion.23 = (bf16[512,1,1312]{0,2,1:T(8,128)(2,1)S(1)}, f32[512,1312]{0,1:T(8,128)}, bf16[512,1,1312]{0,2,1:T(8,128)(2,1)S(1)}) fusion(f32[512,2,1312]{0,2,1:T(8,128)} %fusion.51, bf16[512,1024]{1,0:T(8,128)(2,1)} %all-gather.11.cloned.1.call-done, bf16[1312,1024]{1,0:T(8,128)(2,1)} %param.18), kind=kOutput, calls=%fused_computation.54 | convolution fusion | flops 1427456000 | bytes 14483456 | tf_op jit(solution)/shard_map/dot_general | solution.py:89
  90.1 7.0 fusion.22
  104.3 3.9 reduce-scatter.9.cloned.1.call-done
  112.0 8.6 reduce-scatter.7.cloned.1.call-done
  120.6 3.7 fusion.64
  125.8 8.9 all-gather.13.cloned.1.call-done
  137.3 6.1 fusion.29
  143.4 4.5 multiply_convert_fusion
  150.0 3.9 convolution_bitcast_fusion
  161.3 4.2 bitcast_convert_fusion
  165.6 4.9 convolution_convert_fusion.1
  170.4 4.7 convolution_convert_fusion
  177.1 5.2 convolution_convert_fusion.2
  184.7 44.2 %all-reduce = (f32[1024]{0:T(1024)}, f32[1024]{0:T(1024)}) all-reduce(f32[1024]{0:T(1024)S(1)} %get-tuple-element.54, f32[1024]{0:T(1024)S(1)} %copy-done.25), channel_id=1, replica_groups=mesh['dp'=16,'tensor'=2] {'dp','tensor'}, use_global_device_ids=true, to_apply=%region_16.17 | all-reduce | flops 2048 | bytes 16384 | tf_op jit(solution)/shard_map/psum | solution.py:230
  231.7 225.4 %all-reduce.4.cloned.1.call-done = (bf16[512,1024]{1,0:T(8,128)(2,1)}, bf16[1024,2,1312]{0,2,1:T(8,128)(2,1)}, bf16[1312,1024]{1,0:T(8,128)(2,1)}) async-done(((bf16[512,1024]{1,0:T(8,128)(2,1)}, bf16[1024,2,1312]{0,2,1:T(8,128)(2,1)}, bf16[1312,1024]{1,0:T(8,128)(2,1)}), (bf16[512,1024]{1,0:T(8,128)(2,1)}, bf16[1024,2,1312]{0,2,1:T(8,128)(2,1)}, bf16[1312,1024]{1,0:T(8,128)(2,1)})) %all-reduce.4.cloned.1.call-update) | async-done | bytes 9109520 | tf_op jit(solution)/shard_map/psum | solution.py:233
  463.1 6.5 convert_element_type.136
  469.6 498.3 %all-gather.15.cloned.1.call-done = bf16[16384,3,512]{2,0,1:T(8,128)(2,1)} async-done(((bf16[1024,3,512]{2,0,1:T(8,128)(2,1)}), bf16[16384,3,512]{2,0,1:T(8,128)(2,1)}) %all-gather.15.cloned.1.call-update) | async-done | bytes 50331664 | tf_op jit(solution)/shard_map/all_gather | solution.py:232
  967.9 18.3 %reduce_sum.133 = bf16[1024,3,512]{2,0,1:T(8,128)(2,1)} reduce(bf16[16,1024,3,512]{3,1,0,2:T(8,128)(2,1)} %bitcast.82, bf16[]{:T(256)} %constant.136.clone.1), dimensions={0}, to_apply=%region_17.18 | reduce | flops 23592960 | bytes 53477376 | tf_op jit(solution)/shard_map/reduce_sum | solution.py:232
  986.2 5.5 convert_element_type.132
  (146 shorter events, 67.0 us)
Async XLA Ops:
  7.2 17.4 %copy-start = (bf16[1024,3,512]{2,0,1:T(8,128)(2,1)S(1)}, bf16[1024,3,512]{2,0,1:T(8,128)(2,1)}, u32[]{:S(2)}) copy-start(bf16[1024,3,512]{2,0,1:T(8,128)(2,1)} %param.14) | copy-start | bytes 9437188
  7.2 7.2 copy-start.27
  7.2 17.4 %all-gather.7.cloned.1.call-start = ((), (), s32[]{:S(2)}) async-start(), calls=%async_computation.4 | async-start | bytes 1572864 | tf_op jit(solution)/shard_map/all_gather | solution.py:117
  12.7 38.3 %reduce-scatter.5.cloned.1.call-start = ((), (), s32[]{:S(2)}) async-start(), calls=%async_computation.5 | async-start | bytes 3145728 | tf_op jit(solution)/shard_map/reduce_scatter | solution.py:137
  27.8 5.0 copy-start.14
  39.9 25.7 %all-gather.9.cloned.1.call-start = ((), (), s32[]{:S(2)}) async-start(), calls=%async_computation.6 | async-start | bytes 1572864 | tf_op jit(solution)/shard_map/all_gather | solution.py:145
  55.1 22.1 %all-gather.11.cloned.1.call-start = ((), (), s32[]{:S(2)}) async-start(), calls=%async_computation.8 | async-start | bytes 1572864 | tf_op jit(solution)/shard_map/all_gather | solution.py:162
  55.7 52.6 %reduce-scatter.9.cloned.1.call-start = ((), (), s32[]{:S(2)}) async-start(), calls=%async_computation.9 | async-start | bytes 3145728 | tf_op jit(solution)/shard_map/reduce_scatter | solution.py:173
  97.1 23.4 %reduce-scatter.7.cloned.1.call-start = ((), (), s32[]{:S(2)}) async-start(), calls=%async_computation.7 | async-start | bytes 1572864 | tf_op jit(solution)/shard_map/reduce_scatter | solution.py:153
  97.2 4.3 copy-start.28
  104.3 30.4 %all-gather.13.cloned.1.call-start = ((), (), s32[]{:S(2)}) async-start(), calls=%async_computation.10 | async-start | bytes 1572864 | tf_op jit(solution)/shard_map/all_gather | solution.py:183
  124.3 58.0 %reduce-scatter.11.cloned.1.call-start = ((), (), s32[]{:S(2)}) async-start(), calls=%async_computation.11 | async-start | bytes 1572864 | tf_op jit(solution)/shard_map/reduce_scatter | solution.py:218
  125.8 11.4 %copy-start.26 = (f32[8,512]{1,0:T(8,128)S(1)}, f32[8,512]{1,0:T(8,128)}, u32[]{:S(2)}) copy-start(f32[8,512]{1,0:T(8,128)} %log_add_fusion) | copy-start | bytes 49156
  134.7 8.7 slice-start
  137.3 6.1 slice-start.1
  137.3 6.1 copy-start.15
  165.5 291.6 %all-reduce.4.cloned.1.call-start = ((), (), s32[]{:S(2)}) async-start(), calls=%async_computation.13 | async-start | bytes 18219008 | tf_op jit(solution)/shard_map/psum | solution.py:233
  165.5 4.9 copy-start.29
  165.5 4.9 copy-start.32
  165.6 4.9 copy-start.34
  170.4 4.7 copy-start.13
  170.4 4.7 copy-start.30
  176.8 791.1 %all-gather.15.cloned.1.call-start = ((), (), s32[]{:S(2)}) async-start(), calls=%async_computation.12 | async-start | bytes 53477376 | tf_op jit(solution)/shard_map/all_gather | solution.py:232
  457.1 6.0 slice-start.2
  (25 other events, 46.2 us)
Sparse Core Ops, SparseCore 0:
  12.8 11.7 all-gather.6
  40.0 10.9 reduce-scatter.4
  55.2 10.2 all-gather.8
  66.9 10.1 all-gather.10
  97.3 10.9 reduce-scatter.8
  110.9 9.6 reduce-scatter.6
  124.4 10.2 all-gather.12
  165.6 9.5 reduce-scatter.10
  182.2 274.7 all-reduce.3
  460.2 507.6 all-gather.14
